TPU v7x, 32 devices: a whole 2x2x4 slice. The times are simulated.
32 devices in a mesh: row: 8 (over y, x, core), col: 4 (over z).
Axes of the slice: x: 2, y: 2, z: 4, core: 2. Of those that a mesh axis runs over, the one named last changes fastest.
Arguments:
- matrix: float32 [10240, 10240], P('row', 'col'), may hold values from 0 to 1.5, as said below
Outputs:
- factored: float32 [10240, 10240], P('row', 'col')
Inputs may be any that keep to these rules, and one draw needn't show every extreme that they name: A Gaussian kernel matrix over random embeddings plus a ridge on the diagonal, stored block-cyclically; symmetric positive definite, diagonal entries near 1.5.
All inputs are finite; a program needn't handle non-finite values.
Results may differ from a plain program's by a relative error of at most 0.0003.
Values sent between devices are 32-bit elements; how exact they have to be, the bound alone decides.
A program may use at most 192 MiB of HBM per device.

v0:
```python
import jax
import jax.numpy as jnp
from jax import lax
from jax.sharding import PartitionSpec as P

NB = 256


def spread(array, axis, root):
    mine = lax.axis_index(axis) == root
    return lax.psum(jnp.where(mine, array, jnp.zeros_like(array)), axis)


def make_panel(col_block, k, row_tiles):
    tiles_here = col_block.shape[0] // NB
    diag_block = spread(col_block[:NB], "row", k)
    factor_low = jnp.linalg.cholesky(diag_block)
    inverse = lax.linalg.triangular_solve(
        factor_low, jnp.eye(NB, dtype=factor_low.dtype), left_side=True, lower=True
    )
    scaled = jnp.dot(col_block, inverse.T, precision=lax.Precision.HIGHEST)
    tile_copy = jnp.tile(factor_low, (tiles_here, 1))
    marks = row_tiles[:, None]
    row_panel = jnp.where(marks > k, scaled, jnp.where(marks == k, tile_copy, 0.0))
    return spread(row_panel, "col", k)


def column_panel(row_panel):
    tiles_here = row_panel.shape[0] // NB
    n_row = lax.axis_size("row")
    n_col = lax.axis_size("col")
    groups = n_row // n_col
    pieces = [spread(row_panel, "row", lax.axis_index("col") + m * n_col) for m in range(groups)]
    chosen = jnp.stack(pieces).reshape(groups, tiles_here, NB, NB)
    return chosen.transpose(1, 0, 2, 3).reshape(tiles_here * groups * NB, NB)


def local(matrix):
    local_rows, local_cols = matrix.shape
    n_row = lax.axis_size("row")
    n_col = lax.axis_size("col")
    row_index = lax.axis_index("row")
    col_index = lax.axis_index("col")
    row_tiles = jnp.arange(local_rows, dtype=jnp.int32) // NB * n_row + row_index
    col_tiles = jnp.arange(local_cols, dtype=jnp.int32) // NB * n_col + col_index
    highest = lax.Precision.HIGHEST
    panel_first = make_panel(matrix[:, :NB], 0, row_tiles)
    across_first = column_panel(panel_first)
    rows_first = panel_first * (row_tiles > 0)[:, None]
    cols_first = across_first * (col_tiles > 0)[:, None]
    current = matrix - jnp.dot(rows_first, cols_first.T, precision=highest)
    panel_second = make_panel(current[:, :NB], 1, row_tiles)
    across_second = column_panel(panel_second)
    rows_second = panel_second * (row_tiles > 1)[:, None]
    cols_second = across_second * (col_tiles > 1)[:, None]
    current = current - jnp.dot(rows_second, cols_second.T, precision=highest)
    lead_cols = current[:, :NB]
    lead_cols = jnp.where(col_index == 0, panel_first, lead_cols)
    lead_cols = jnp.where(col_index == 1, panel_second, lead_cols)
    current = current.at[:, :NB].set(lead_cols)
    zero_mask = (row_tiles[:, None] == 0) & (col_tiles[None, :] > 0) | (row_tiles[:, None] == 1) & (
        col_tiles[None, :] > 1
    )
    return jnp.where(zero_mask, 0.0, current)


def solution(mesh):
    placed = (P("row", "col"),)
    return jax.shard_map(
        local, mesh=mesh, in_specs=placed, out_specs=P("row", "col"), check_vma=False
    )
```

profile of v0, /device:TPU:0, one launch (start us, length us, event | category | flops | bytes accessed | tf_op | source)
XLA Modules:
  0.0 600.5 jit_solution(3242503386733762147)
XLA Ops:
  6.5 13.9 %copy.18 = f32[1280,2560]{0,1:T(8,128)} copy(f32[1280,2560]{1,0:T(8,128)} %param.6) | data formatting | bytes 26214400 | tf_op args[0]
  20.4 1.7 slice_select_fusion.1
  22.2 56.6 %all-reduce.10.cloned.1.call-done = f32[256,256]{0,1:T(8,128)} async-done(((f32[256,256]{0,1:T(8,128)}), f32[256,256]{0,1:T(8,128)}) %all-reduce.10.cloned.1.call-update) | async-done | bytes 262160 | tf_op jit(solution)/shard_map/psum | solution.py:11
  78.8 1.1 copy.13
  79.9 1.0 fusion.16
  80.9 11.7 %cholesky.130 = f32[128,128]{1,0:T(8,128)S(1)} custom-call(f32[128,128]{1,0:T(8,128)S(1)} %cholesky.194), custom_call_target="Cholesky" | custom-call | tf_op jit(solution)/shard_map/jit(cholesky)/cholesky | solution.py:17
  92.7 9.8 %custom-call.13 = f32[1,128,128]{1,2,0:T(8,128)S(1)} custom-call(f32[1,128,128]{2,1,0:T(8,128)S(1)} %get-tuple-element.74), custom_call_target="InvertDiagBlocksLowerTriangular" | custom-call | tf_op jit(solution)/shard_map/jit(cholesky)/cholesky | solution.py:17
  102.7 0.3 convolution_subtract_fusion.5
  103.0 11.7 %cholesky.147 = f32[128,128]{1,0:T(8,128)S(1)} custom-call(f32[128,128]{1,0:T(8,128)S(1)} %convolution_subtract_fusion.5), custom_call_target="Cholesky" | custom-call | tf_op jit(solution)/shard_map/jit(cholesky)/cholesky | solution.py:17
  114.8 0.7 compare_reduce_fusion.2
  116.9 4.6 while.5
  117.4 0.7 fusion.72
  118.1 1.3 bitcast_dynamic-update-slice_fusion.4
  119.4 0.7 fusion.72
  120.1 1.3 bitcast_dynamic-update-slice_fusion.4
  121.5 19.7 %custom-call.14 = f32[2,128,128]{1,2,0:T(8,128)S(1)} custom-call(f32[2,128,128]{2,1,0:T(8,128)S(1)} %get-tuple-element.33), custom_call_target="InvertDiagBlocksLowerTriangular" | custom-call | tf_op jit(solution)/shard_map/triangular_solve/custom-call.0 | solution.py:18
  141.1 0.3 fusion.23
  141.7 0.3 fusion.30
  142.2 0.4 copy.14
  142.6 3.7 fusion.2
  146.3 59.6 %all-reduce.12.cloned.1.call-done = f32[1280,256]{0,1:T(8,128)} async-done(((f32[1280,256]{0,1:T(8,128)}), f32[1280,256]{0,1:T(8,128)}) %all-reduce.12.cloned.1.call-update) | async-done | bytes 1310736 | tf_op jit(solution)/shard_map/psum | solution.py:11
  205.9 1.5 broadcast_select_fusion.2
  207.4 1.5 copy.15
  208.9 1.5 copy.16
  210.5 64.3 %all-reduce.20.cloned.1.call-done = (f32[1,5,256,256]{3,2,1,0:T(8,128)}, f32[1,5,256,256]{3,2,1,0:T(8,128)}) async-done(((f32[1,5,256,256]{3,2,1,0:T(8,128)}, f32[1,5,256,256]{3,2,1,0:T(8,128)}), (f32[1,5,256,256]{3,2,1,0:T(8,128)}, f32[1,5,256,256]{3,2,1,0:T(8,128)})) %all-reduce.20.cloned.1.call-update) | async-done | bytes 2621456 | tf_op jit(solution)/shard_map/psum | solution.py:11
  274.8 2.0 maximum_bitcast_fusion
  277.1 0.4 bitcast_multiply_fusion.1
  277.5 0.9 copy-done.1
  278.4 15.0 %convolution_subtract_fusion.1 = f32[1280,2560]{0,1:T(8,128)S(1)} fusion(f32[1280,2560]{0,1:T(8,128)} %copy.18, f32[2560,256]{1,0:T(8,128)S(1)} %bitcast_multiply_fusion.1, f32[1280,256]{0,1:T(8,128)S(1)} %copy-done.1, f32[1280]{0:T(1024)S(1)} %fusion.53), kind=kOutput, calls=%fused_computation.5 | convolution fusion | flops 10069934080 | bytes 30151680 | tf_op jit(solution)/shard_map/dot_general | solution.py:51
  293.4 4.9 copy-done
  298.3 0.7 slice_select_fusion
  299.3 53.3 %all-reduce.14.cloned.1.call-done = f32[256,256]{0,1:T(8,128)} async-done(((f32[256,256]{0,1:T(8,128)}), f32[256,256]{0,1:T(8,128)}) %all-reduce.14.cloned.1.call-update) | async-done | bytes 262160 | tf_op jit(solution)/shard_map/psum | solution.py:11
  352.7 1.1 copy.20
  353.7 1.0 fusion.15
  354.7 11.7 %cholesky.164 = f32[128,128]{1,0:T(8,128)S(1)} custom-call(f32[128,128]{1,0:T(8,128)S(1)} %cholesky.197), custom_call_target="Cholesky" | custom-call | tf_op jit(solution)/shard_map/jit(cholesky)/cholesky | solution.py:17
  366.5 9.8 %custom-call.15 = f32[1,128,128]{1,2,0:T(8,128)S(1)} custom-call(f32[1,128,128]{2,1,0:T(8,128)S(1)} %get-tuple-element.70), custom_call_target="InvertDiagBlocksLowerTriangular" | custom-call | tf_op jit(solution)/shard_map/jit(cholesky)/cholesky | solution.py:17
  376.5 0.3 convolution_subtract_fusion.4
  376.8 11.7 %cholesky.181 = f32[128,128]{1,0:T(8,128)S(1)} custom-call(f32[128,128]{1,0:T(8,128)S(1)} %convolution_subtract_fusion.4), custom_call_target="Cholesky" | custom-call | tf_op jit(solution)/shard_map/jit(cholesky)/cholesky | solution.py:17
  388.6 0.6 compare_reduce_fusion
  389.2 0.7 compare_reduce_fusion.1
  391.2 4.3 while.6
  391.5 0.7 fusion.73
  392.1 1.3 bitcast_dynamic-update-slice_fusion.5
  393.5 0.7 fusion.73
  394.2 1.3 bitcast_dynamic-update-slice_fusion.5
  395.5 19.7 %custom-call.16 = f32[2,128,128]{1,2,0:T(8,128)S(1)} custom-call(f32[2,128,128]{2,1,0:T(8,128)S(1)} %get-tuple-element.34), custom_call_target="InvertDiagBlocksLowerTriangular" | custom-call | tf_op jit(solution)/shard_map/triangular_solve/custom-call.0 | solution.py:18
  415.2 0.3 fusion.21
  415.8 0.3 fusion.26
  416.1 1.2 tile.20
  417.3 1.7 copy.21
  419.0 3.7 fusion
  422.8 59.6 %all-reduce.16.cloned.1.call-done = f32[1280,256]{0,1:T(8,128)} async-done(((f32[1280,256]{0,1:T(8,128)}), f32[1280,256]{0,1:T(8,128)}) %all-reduce.16.cloned.1.call-update) | async-done | bytes 1310736 | tf_op jit(solution)/shard_map/psum | solution.py:11
  482.4 2.6 broadcast_select_fusion.3
  485.0 2.8 copy.23
  487.8 1.5 copy.24
  489.3 0.9 compare_reduce_fusion.4
  490.3 63.5 %all-reduce.18.cloned.1.call-done = (f32[1,5,256,256]{3,2,1,0:T(8,128)}, f32[1,5,256,256]{3,2,1,0:T(8,128)}) async-done(((f32[1,5,256,256]{3,2,1,0:T(8,128)}, f32[1,5,256,256]{3,2,1,0:T(8,128)}), (f32[1,5,256,256]{3,2,1,0:T(8,128)}, f32[1,5,256,256]{3,2,1,0:T(8,128)})) %all-reduce.18.cloned.1.call-update) | async-done | bytes 2621456 | tf_op jit(solution)/shard_map/psum | solution.py:11
  553.7 2.0 maximum_bitcast_fusion.1
  556.0 0.4 bitcast_multiply_fusion
  556.4 0.9 copy-done.2
  557.3 15.0 %convolution_subtract_fusion = f32[1280,2560]{0,1:T(8,128)S(1)} fusion(f32[1280,2560]{0,1:T(8,128)} %copy-done, f32[2560,256]{1,0:T(8,128)S(1)} %bitcast_multiply_fusion, f32[1280,256]{0,1:T(8,128)S(1)} %copy-done.2, f32[1280]{0:T(1024)S(1)} %fusion.54), kind=kOutput, calls=%fused_computation.4 | convolution fusion | flops 10069934080 | bytes 30151680 | tf_op jit(solution)/shard_map/dot_general | solution.py:56
  572.3 1.3 select_dynamic-update-slice_fusion
  573.6 5.9 or_select_fusion
  579.5 13.9 %copy.27 = f32[1280,2560]{1,0:T(8,128)} copy(f32[1280,2560]{0,1:T(8,128)} %or_select_fusion) | data formatting | bytes 26214400 | tf_op jit(solution)/shard_map/jit(_where)/select_n | solution.py:64
  (48 shorter events, 2.4 us)
Async XLA Ops:
  6.5 72.3 %all-reduce.10.cloned.1.call-start = ((), (), s32[]{:S(2)}) async-start(), calls=%async_computation | async-start | bytes 524288 | tf_op jit(solution)/shard_map/psum | solution.py:11
  22.1 183.8 %all-reduce.12.cloned.1.call-start = ((), (), s32[]{:S(2)}) async-start(), calls=%async_computation.1 | async-start | bytes 2621440 | tf_op jit(solution)/shard_map/psum | solution.py:11
  146.3 128.6 %all-reduce.20.cloned.1.call-start = ((), (), s32[]{:S(2)}) async-start(), calls=%async_computation.5 | async-start | bytes 5242880 | tf_op jit(solution)/shard_map/psum | solution.py:11
  210.4 142.2 %all-reduce.14.cloned.1.call-start = ((), (), s32[]{:S(2)}) async-start(), calls=%async_computation.2 | async-start | bytes 524288 | tf_op jit(solution)/shard_map/psum | solution.py:11
  277.0 1.3 copy-start.1
  293.4 5.0 copy-start
  299.1 183.3 %all-reduce.16.cloned.1.call-start = ((), (), s32[]{:S(2)}) async-start(), calls=%async_computation.3 | async-start | bytes 2621440 | tf_op jit(solution)/shard_map/psum | solution.py:11
  422.8 131.0 %all-reduce.18.cloned.1.call-start = ((), (), s32[]{:S(2)}) async-start(), calls=%async_computation.4 | async-start | bytes 5242880 | tf_op jit(solution)/shard_map/psum | solution.py:11
  555.9 1.3 copy-start.2
Sparse Core Ops, SparseCore 0:
  22.2 56.5 all-reduce.9
  146.4 59.4 all-reduce.11
  210.6 64.2 all-reduce.19
  299.2 53.4 all-reduce.13
  422.9 59.4 all-reduce.15
  489.4 64.2 all-reduce.17
where the time goes:
time: 610 us; the launch traced here: 601 us
  waiting for transfers between devices  357 us (59%)
  other arithmetic  130 us (21%)
  local copies, waits for them, and re-layouts  55.9 us (9%)
  matrix products  40.2 us (7%)
  between operations  16.7 us (3%)
    psum x6, waiting for transfers between devices, spread(): return lax.psum(jnp.where(mine, array, jnp.zeros_like(array)), axis)  357 us
    another operation x13, other arithmetic, make_panel(): factor_low = jnp.linalg.cholesky(diag_block)  68.7 us
    another operation x5, other arithmetic, make_panel(): lax.linalg.triangular_solve(factor_low, jnp.eye(NB, dtype=factor_low.dtyp...  39.4 us
    unnamed x7, local copies, waits for them, and re-layouts  20.6 us
    dot_general x1, matrix products, local(): current = matrix - jnp.dot(rows_first, cols_first.T, precision=highest)  15 us
    dot_general x1, matrix products, local(): current = current - jnp.dot(rows_second, cols_second.T, precision=highest)  15 us
    select_n x1, local copies, waits for them, and re-layouts, local(): return jnp.where(zero_mask, 0.0, current)  13.9 us
  transfers between devices with their start and end apart: 6, of which 6 were waited for; matrix products, arithmetic and copies ran while one was open for 0% of the time, Pallas kernels for 0%

commit v1 on v0

--- a/solution.py
+++ b/solution.py
@@ -6,9 +6,15 @@
 NB = 256
 
 
+def add_all(shard, name):
+    parts = lax.all_gather(shard, name, axis=0, tiled=False)
+    summed = parts.sum(axis=0)
+    return summed
+
+
 def spread(array, axis, root):
     mine = lax.axis_index(axis) == root
-    return lax.psum(jnp.where(mine, array, jnp.zeros_like(array)), axis)
+    return add_all(jnp.where(mine, array, jnp.zeros_like(array)), axis)
 
 
 def make_panel(col_block, k, row_tiles):

time: 610 us -> 809 us (1.33)
  waiting for transfers between devices: 357 us -> 478 us
  local copies, waits for them, and re-layouts: 55.9 us -> 110 us
  other arithmetic: 130 us -> 153 us
    all_gather x0 -> x8, waiting for transfers between devices: none -> 476 us  [add_all(): parts = lax.all_gather(shard, name, axis=0, tiled=False)]
    psum x6 -> x0, waiting for transfers between devices: 357 us -> none  [spread(): return lax.psum(jnp.where(mine, array, jnp.zeros_like(array)), axis)]
    unnamed x7 -> x17, local copies, waits for them, and re-layouts: 20.6 us -> 58.5 us
    reduce_sum x0 -> x8, other arithmetic: none -> 26.5 us  [add_all(): summed = parts.sum(axis=0)]
    all_gather x0 -> x2, local copies, waits for them, and re-layouts: none -> 14.4 us  [add_all(): parts = lax.all_gather(shard, name, axis=0, tiled=False)]
    reduce_sum x0 -> x6, local copies, waits for them, and re-layouts: none -> 11.7 us  [add_all(): summed = parts.sum(axis=0)]
  transfers between devices with their start and end apart: 6 -> 8, of which waited for: 6 -> 8; matrix products, arithmetic and copies ran while one was open for 0% -> 4% of each run, Pallas kernels for 0% -> 0%
where the time goes in v1:
time: 809 us; the launch traced here: 799 us
  waiting for transfers between devices  478 us (59%)
  other arithmetic  153 us (19%)
  local copies, waits for them, and re-layouts  110 us (14%)
  matrix products  40.2 us (5%)
  between operations  16.6 us (2%)
    all_gather x8, waiting for transfers between devices, add_all(): parts = lax.all_gather(shard, name, axis=0, tiled=False)  476 us
    another operation x13, other arithmetic, make_panel(): factor_low = jnp.linalg.cholesky(diag_block)  68.7 us
    unnamed x17, local copies, waits for them, and re-layouts  58.5 us
    another operation x5, other arithmetic, make_panel(): lax.linalg.triangular_solve(factor_low, jnp.eye(NB, dtype=factor_low.dtyp...  39.4 us
    reduce_sum x8, other arithmetic, add_all(): summed = parts.sum(axis=0)  26.5 us
  transfers between devices with their start and end apart: 8, of which 8 were waited for; matrix products, arithmetic and copies ran while one was open for 4% of the time, Pallas kernels for 0%

profile of v1, /device:TPU:0, one launch (start us, length us, event | category | flops | bytes accessed | tf_op | source)
XLA Modules:
  0.0 798.7 jit_solution(5499515363278939882)
XLA Ops:
  6.5 13.9 %copy.42 = f32[1280,2560]{0,1:T(8,128)} copy(f32[1280,2560]{1,0:T(8,128)} %param.6) | data formatting | bytes 26214400 | tf_op args[0]
  20.4 1.7 slice_select_fusion.1
  22.3 30.9 %all-gather.17.cloned.1.call-done = f32[2048,256]{0,1:T(8,128)} async-done(((f32[256,256]{0,1:T(8,128)}), f32[2048,256]{0,1:T(8,128)}) %all-gather.17.cloned.1.call-update) | async-done | bytes 2097168 | tf_op jit(solution)/shard_map/all_gather | solution.py:10
  53.1 2.5 copy.55
  56.3 11.7 %cholesky.130 = f32[128,128]{1,0:T(8,128)S(1)} custom-call(f32[128,128]{1,0:T(8,128)S(1)} %cholesky.194), custom_call_target="Cholesky" | custom-call | tf_op jit(solution)/shard_map/jit(cholesky)/cholesky | solution.py:23
  68.1 9.8 %custom-call.13 = f32[1,128,128]{1,2,0:T(8,128)S(1)} custom-call(f32[1,128,128]{2,1,0:T(8,128)S(1)} %get-tuple-element.70), custom_call_target="InvertDiagBlocksLowerTriangular" | custom-call | tf_op jit(solution)/shard_map/jit(cholesky)/cholesky | solution.py:23
  78.4 11.7 %cholesky.147 = f32[128,128]{1,0:T(8,128)S(1)} custom-call(f32[128,128]{1,0:T(8,128)S(1)} %convolution_subtract_fusion.5), custom_call_target="Cholesky" | custom-call | tf_op jit(solution)/shard_map/jit(cholesky)/cholesky | solution.py:23
  90.2 0.7 compare_reduce_fusion.2
  92.3 4.2 while.5
  92.5 0.7 fusion.72
  93.1 1.3 bitcast_dynamic-update-slice_fusion.4
  94.5 0.7 fusion.72
  95.2 1.3 bitcast_dynamic-update-slice_fusion.4
  96.5 19.7 %custom-call.14 = f32[2,128,128]{1,2,0:T(8,128)S(1)} custom-call(f32[2,128,128]{2,1,0:T(8,128)S(1)} %get-tuple-element.33), custom_call_target="InvertDiagBlocksLowerTriangular" | custom-call | tf_op jit(solution)/shard_map/triangular_solve/custom-call.0 | solution.py:24
  117.6 3.7 fusion.2
  121.4 98.1 %all-gather.19.cloned.1.call-done = f32[5120,256]{0,1:T(8,128)} async-done(((f32[1280,256]{0,1:T(8,128)}), f32[5120,256]{0,1:T(8,128)}) %all-gather.19.cloned.1.call-update) | async-done | bytes 5242896 | tf_op jit(solution)/shard_map/all_gather | solution.py:10
  219.6 7.2 reshape.215
  226.8 5.6 reduce_sum.73
  232.4 1.7 broadcast_select_fusion.2
  234.9 60.7 %all-gather.21.cloned.1.call-done = f32[10240,256]{0,1:T(8,128)} async-done(((f32[1280,256]{0,1:T(8,128)}), f32[10240,256]{0,1:T(8,128)}) %all-gather.21.cloned.1.call-update) | async-done | bytes 10485776 | tf_op jit(solution)/shard_map/all_gather | solution.py:10
  295.7 8.3 %copy.56 = f32[32,8,8,1280]{3,2,1,0:T(8,128)S(1)} copy(f32[32,8,8,1280]{3,1,2,0:T(8,128)} %bitcast.120) | data formatting | bytes 20971520
  304.0 3.6 bitcast_reduce_fusion.3
  307.5 2.8 copy.39
  310.3 50.3 %all-gather.23.cloned.1.call-done = f32[10240,256]{0,1:T(8,128)} async-done(((f32[1280,256]{0,1:T(8,128)}), f32[10240,256]{0,1:T(8,128)}) %all-gather.23.cloned.1.call-update) | async-done | bytes 10485776 | tf_op jit(solution)/shard_map/all_gather | solution.py:10
  360.6 8.7 %copy.57 = f32[32,8,8,1280]{3,2,1,0:T(8,128)S(1)} copy(f32[32,8,8,1280]{3,1,2,0:T(8,128)} %bitcast.121) | data formatting | bytes 20971520
  369.3 3.5 bitcast_reduce_fusion.2
  372.8 2.9 copy.40
  375.7 1.5 maximum_bitcast_fusion
  377.9 15.0 %convolution_subtract_fusion.1 = f32[1280,2560]{0,1:T(8,128)S(1)} fusion(f32[1280,2560]{0,1:T(8,128)} %copy.42, f32[2560,256]{1,0:T(8,128)S(1)} %bitcast_multiply_fusion.1, f32[1280,256]{0,1:T(8,128)S(1)} %reduce_sum.73, f32[1280]{0:T(1024)S(1)} %fusion.53), kind=kOutput, calls=%fused_computation.5 | convolution fusion | flops 10069934080 | bytes 30151680 | tf_op jit(solution)/shard_map/dot_general | solution.py:57
  392.9 4.9 copy-done
  397.9 0.7 slice_select_fusion
  398.9 28.0 %all-gather.25.cloned.1.call-done = f32[2048,256]{0,1:T(8,128)} async-done(((f32[256,256]{0,1:T(8,128)}), f32[2048,256]{0,1:T(8,128)}) %all-gather.25.cloned.1.call-update) | async-done | bytes 2097168 | tf_op jit(solution)/shard_map/all_gather | solution.py:10
  426.9 2.5 copy.58
  430.1 11.7 %cholesky.164 = f32[128,128]{1,0:T(8,128)S(1)} custom-call(f32[128,128]{1,0:T(8,128)S(1)} %cholesky.197), custom_call_target="Cholesky" | custom-call | tf_op jit(solution)/shard_map/jit(cholesky)/cholesky | solution.py:23
  441.9 9.8 %custom-call.15 = f32[1,128,128]{1,2,0:T(8,128)S(1)} custom-call(f32[1,128,128]{2,1,0:T(8,128)S(1)} %get-tuple-element.66), custom_call_target="InvertDiagBlocksLowerTriangular" | custom-call | tf_op jit(solution)/shard_map/jit(cholesky)/cholesky | solution.py:23
  452.2 11.7 %cholesky.181 = f32[128,128]{1,0:T(8,128)S(1)} custom-call(f32[128,128]{1,0:T(8,128)S(1)} %convolution_subtract_fusion.4), custom_call_target="Cholesky" | custom-call | tf_op jit(solution)/shard_map/jit(cholesky)/cholesky | solution.py:23
  464.5 0.7 compare_reduce_fusion.1
  466.6 4.3 while.6
  467.5 1.3 bitcast_dynamic-update-slice_fusion.5
  469.5 1.3 bitcast_dynamic-update-slice_fusion.5
  470.9 19.7 %custom-call.16 = f32[2,128,128]{1,2,0:T(8,128)S(1)} custom-call(f32[2,128,128]{2,1,0:T(8,128)S(1)} %get-tuple-element.34), custom_call_target="InvertDiagBlocksLowerTriangular" | custom-call | tf_op jit(solution)/shard_map/triangular_solve/custom-call.0 | solution.py:24
  491.5 1.2 tile.20
  492.6 1.7 copy.45
  494.3 3.8 fusion
  498.2 98.1 %all-gather.27.cloned.1.call-done = f32[5120,256]{0,1:T(8,128)} async-done(((f32[1280,256]{0,1:T(8,128)}), f32[5120,256]{0,1:T(8,128)}) %all-gather.27.cloned.1.call-update) | async-done | bytes 5242896 | tf_op jit(solution)/shard_map/all_gather | solution.py:10
  596.3 7.2 reshape.219
  603.5 5.6 reduce_sum.77
  609.1 1.8 broadcast_select_fusion.3
  611.0 0.7 all-gather.31.cloned.1.call-update
  611.8 1.0 compare_reduce_fusion.4
  612.8 59.7 %all-gather.29.cloned.1.call-done = f32[10240,256]{0,1:T(8,128)} async-done(((f32[1280,256]{0,1:T(8,128)}), f32[10240,256]{0,1:T(8,128)}) %all-gather.29.cloned.1.call-update) | async-done | bytes 10485776 | tf_op jit(solution)/shard_map/all_gather | solution.py:10
  672.6 8.3 %copy.59 = f32[32,8,8,1280]{3,2,1,0:T(8,128)S(1)} copy(f32[32,8,8,1280]{3,1,2,0:T(8,128)} %bitcast.118) | data formatting | bytes 20971520
  680.9 3.6 bitcast_reduce_fusion.1
  684.4 2.8 copy.47
  687.2 50.4 %all-gather.31.cloned.1.call-done = f32[10240,256]{0,1:T(8,128)} async-done(((f32[1280,256]{0,1:T(8,128)}), f32[10240,256]{0,1:T(8,128)}) %all-gather.31.cloned.1.call-update) | async-done | bytes 10485776 | tf_op jit(solution)/shard_map/all_gather | solution.py:10
  737.6 8.5 %copy.60 = f32[32,8,8,1280]{3,2,1,0:T(8,128)S(1)} copy(f32[32,8,8,1280]{3,1,2,0:T(8,128)} %bitcast.119) | data formatting | bytes 20971520
  746.1 3.5 bitcast_reduce_fusion
  749.6 2.9 copy.48
  752.6 1.5 maximum_bitcast_fusion.1
  754.7 0.9 copy-done.2
  755.6 15.0 %convolution_subtract_fusion = f32[1280,2560]{0,1:T(8,128)S(1)} fusion(f32[1280,2560]{0,1:T(8,128)} %copy-done, f32[2560,256]{1,0:T(8,128)S(1)} %bitcast_multiply_fusion, f32[1280,256]{0,1:T(8,128)S(1)} %copy-done.2, f32[1280]{0:T(1024)S(1)} %fusion.54), kind=kOutput, calls=%fused_computation.4 | convolution fusion | flops 10069934080 | bytes 30151680 | tf_op jit(solution)/shard_map/dot_general | solution.py:62
  770.6 1.2 select_dynamic-update-slice_fusion
  771.9 5.9 or_select_fusion
  777.8 13.9 %copy.51 = f32[1280,2560]{1,0:T(8,128)} copy(f32[1280,2560]{0,1:T(8,128)} %or_select_fusion) | data formatting | bytes 26214400 | tf_op jit(solution)/shard_map/jit(_where)/select_n | solution.py:70
  (74 shorter events, 9.6 us)
Async XLA Ops:
  6.5 46.6 %all-gather.17.cloned.1.call-start = ((), (), s32[]{:S(2)}) async-start(), calls=%async_computation | async-start | bytes 2359296 | tf_op jit(solution)/shard_map/all_gather | solution.py:10
  22.2 197.4 %all-gather.19.cloned.1.call-start = ((), (), s32[]{:S(2)}) async-start(), calls=%async_computation.1 | async-start | bytes 6553600 | tf_op jit(solution)/shard_map/all_gather | solution.py:10
  121.4 174.3 %all-gather.21.cloned.1.call-start = ((), (), s32[]{:S(2)}) async-start(), calls=%async_computation.2 | async-start | bytes 11796480 | tf_op jit(solution)/shard_map/all_gather | solution.py:10
  234.1 126.5 %all-gather.23.cloned.1.call-start = ((), (), s32[]{:S(2)}) async-start(), calls=%async_computation.3 | async-start | bytes 11796480 | tf_op jit(solution)/shard_map/all_gather | solution.py:10
  234.6 192.3 %all-gather.25.cloned.1.call-start = ((), (), s32[]{:S(2)}) async-start(), calls=%async_computation.4 | async-start | bytes 2359296 | tf_op jit(solution)/shard_map/all_gather | solution.py:10
  372.8 2.9 copy-start.3
  392.9 5.0 copy-start
  398.6 197.7 %all-gather.27.cloned.1.call-start = ((), (), s32[]{:S(2)}) async-start(), calls=%async_computation.5 | async-start | bytes 6553600 | tf_op jit(solution)/shard_map/all_gather | solution.py:10
  498.1 174.4 %all-gather.29.cloned.1.call-start = ((), (), s32[]{:S(2)}) async-start(), calls=%async_computation.6 | async-start | bytes 11796480 | tf_op jit(solution)/shard_map/all_gather | solution.py:10
  609.1 1.9 copy-start.1
  611.0 126.6 %all-gather.31.cloned.1.call-start = ((), (), s32[]{:S(2)}) async-start(), calls=%async_computation.7 | async-start | bytes 11796480 | tf_op jit(solution)/shard_map/all_gather | solution.py:10
  749.6 2.9 copy-start.4
  754.3 1.3 copy-start.2
Sparse Core Ops, SparseCore 0:
  22.3 30.8 all-gather.16
  121.5 98.0 all-gather.18
  234.2 61.4 all-gather.20
  297.4 63.1 all-gather.22
  398.7 28.0 all-gather.24
  498.3 98.0 all-gather.26
  611.1 61.4 all-gather.28
  674.5 63.1 all-gather.30
